TPU v7x, 32 devices: a whole 2x2x4 slice. The times are simulated.
32 devices in a mesh: groups: 2 (over x), lon: 16 (over z, y, core).
Axes of the slice: x: 2, y: 2, z: 4, core: 2. Of those that a mesh axis runs over, the one named last changes fastest.
Arguments:
- fields: bfloat16 [32, 32, 1500], P(('groups', 'lon')), parts along dimension 0, may hold values from -6 to 6
- level_ids: int32 [6], P('groups'), parts along dimension 0, may hold values from 0 to 2, each once
- embed_weight: bfloat16 [500, 512], replicated, may hold values from -0.25 to 0.25
- level_embed: bfloat16 [3, 512], replicated, may hold values from -6 to 6
- enc_gain: float32 [512], replicated, may hold values from 0.1 to 1.9
- latent_query: bfloat16 [2, 512], replicated, may hold values from -0.049804688 to 0.049804688
- kv_weight: bfloat16 [512, 1024], replicated, may hold values from -0.25 to 0.25
- pool_out: bfloat16 [512, 512], replicated, may hold values from -0.25 to 0.25
- attn_gain: float32 [512], replicated, may hold values from 0.1 to 1.9
- qkv_weight: bfloat16 [512, 1536], replicated, may hold values from -0.25 to 0.25
- attn_proj: bfloat16 [512, 512], replicated, may hold values from -0.25 to 0.25
- mlp_gain: float32 [512], replicated, may hold values from 0.1 to 1.9
- mlp_up: bfloat16 [512, 2048], replicated, may hold values from -0.25 to 0.25
- mlp_down: bfloat16 [2048, 512], replicated, may hold values from -0.125 to 0.125
- level_mix: float32 [3, 2], replicated, may hold values from 0.25 to 4
- dec_gain: float32 [512], replicated, may hold values from 0.1 to 1.9
- dec_weight: bfloat16 [512, 500], replicated, may hold values from -0.25 to 0.25
Outputs:
- forecast: bfloat16 [32, 32, 1500], P(('groups', 'lon')), parts along dimension 0
There are 2 independent parts, one for each index of `groups`. A program takes and returns all parts, laid end to end along the dimension named above; an argument that names none is the same for every part. Nothing has to cross between parts.
Inputs may be any that keep to these rules, and one draw needn't show every extreme that they name: level_ids holds each of 0 to 2 once.
All inputs are finite; a program needn't handle non-finite values.
Results may differ from a plain program's by a relative error of at most 0.014.
Values may be sent and summed in bfloat16 or wider, within the bound.
A program may use at most 128 MiB of HBM per device.

v0:
```python
import jax
import jax.numpy as jnp
from jax import lax
from jax.sharding import PartitionSpec as P

D = 512
HEADS = 8
PIN = 500
LEV = 3
LATL = 2
W_LAT = 4
W_LON = 8
STEPS = 2
ROW_PARTS = 4
norm_eps = 1e-05
head_eps = 1e-06


def product(einsum_form, left_side, right_side):
    return jnp.einsum(einsum_form, left_side, right_side, preferred_element_type=jnp.float32)


def layer_norm(values, scale_row):
    average = jnp.mean(values, axis=-1, keepdims=True)
    centred = values - average
    spread = jnp.mean(centred * centred, axis=-1, keepdims=True)
    return centred * lax.rsqrt(spread + norm_eps) * scale_row


def unit_heads(values):
    shaped = values.reshape(values.shape[:-1] + (HEADS, D // HEADS))
    mean_square = jnp.mean(shaped * shaped, axis=-1, keepdims=True)
    return (shaped * lax.rsqrt(mean_square + head_eps)).reshape(values.shape)


def level_tables(level_ids, level_embed, level_mix):
    picker = (level_ids[:, None] == jnp.arange(LEV, dtype=jnp.int32)[None, :]).astype(jnp.float32)
    embeds = jnp.dot(picker, level_embed.astype(jnp.float32), precision=lax.Precision.HIGHEST)
    mixing = jnp.dot(picker, level_mix, precision=lax.Precision.HIGHEST)
    return (embeds, mixing)


def head_tables(queries):
    head_dim = D // HEADS
    feature_head = jnp.arange(D, dtype=jnp.int32) // head_dim
    head_ids = jnp.arange(HEADS, dtype=jnp.int32)
    spreader = (head_ids[:, None] == feature_head[None, :]).astype(jnp.bfloat16)
    on_head = (feature_head[:, None] == head_ids[None, :]).astype(jnp.bfloat16)
    query_table = (queries.T[:, :, None] * on_head[:, None, :]).reshape(D, LATL * HEADS)
    return (query_table, spreader)


def encode(
    flat_fields,
    embeds,
    query_table,
    spreader,
    embed_weight,
    enc_gain,
    kv_weight,
    pool_out,
    latent_query,
):
    head_dim = D // HEADS
    patch_count = flat_fields.shape[0]
    patches = flat_fields.reshape(patch_count * LEV, PIN)
    tokens = jnp.dot(patches, embed_weight, preferred_element_type=jnp.float32).reshape(
        patch_count, LEV, D
    )
    tokens = layer_norm(tokens + embeds[None], enc_gain).astype(jnp.bfloat16)
    keyval = jnp.dot(
        tokens.reshape(patch_count * LEV, D), kv_weight, preferred_element_type=jnp.float32
    )
    key_rows = unit_heads(keyval[:, :D]).astype(jnp.bfloat16)
    value_rows = keyval[:, D:].astype(jnp.bfloat16).reshape(patch_count, LEV, 1, D)
    scores = jnp.dot(key_rows, query_table, preferred_element_type=jnp.float32) * head_dim ** (-0.5)
    scores = scores.reshape(patch_count, LEV, LATL * HEADS)
    weights = jnp.exp(scores)
    weights = (weights / jnp.sum(weights, axis=1, keepdims=True)).astype(jnp.bfloat16)
    spread_weights = jnp.dot(
        weights.reshape(patch_count * LEV * LATL, HEADS),
        spreader,
        preferred_element_type=jnp.float32,
    )
    spread_weights = spread_weights.reshape(patch_count, LEV, LATL, D)
    pooled = jnp.sum(spread_weights * value_rows.astype(jnp.float32), axis=1)
    pooled = pooled.astype(jnp.bfloat16).reshape(patch_count * LATL, D)
    latents = jnp.dot(pooled, pool_out, preferred_element_type=jnp.float32).reshape(
        patch_count, LATL, D
    )
    return (latents + latent_query.astype(jnp.float32)[None]).astype(jnp.bfloat16)


def increments(backbone_out, embeds, mixing, dec_gain, dec_weight):
    patch_count = backbone_out.shape[0]
    blended = mixing[None, :, 0, None] * backbone_out[:, None, 0, :].astype(jnp.float32)
    blended = blended + mixing[None, :, 1, None] * backbone_out[:, None, 1, :].astype(jnp.float32)
    blended = blended + embeds[None]
    normed = layer_norm(blended, dec_gain).astype(jnp.bfloat16)
    result = jnp.dot(
        normed.reshape(patch_count * LEV, D), dec_weight, preferred_element_type=jnp.float32
    )
    return result.astype(jnp.bfloat16).reshape(patch_count, LEV * PIN)


def window_block(shifted, attn_gain, qkv_weight, attn_proj):
    head_dim = D // HEADS
    lat_count, lon_count = (shifted.shape[0], shifted.shape[1])
    lat_win, lon_win = (lat_count // W_LAT, lon_count // W_LON)
    inside = W_LAT * W_LON * LATL
    flat_tokens = shifted.reshape(-1, D)
    normed = layer_norm(flat_tokens.astype(jnp.float32), attn_gain).astype(jnp.bfloat16)
    projected = jnp.dot(normed, qkv_weight, preferred_element_type=jnp.float32)
    query_heads = unit_heads(projected[:, :D]).astype(jnp.bfloat16)
    key_heads = unit_heads(projected[:, D : 2 * D]).astype(jnp.bfloat16)
    value_heads = projected[:, 2 * D :].astype(jnp.bfloat16)

    def to_windows(head_data):
        shaped = head_data.reshape(lat_win, W_LAT, lon_win, W_LON, LATL, HEADS, head_dim)
        return shaped.transpose(0, 2, 5, 1, 3, 4, 6).reshape(
            lat_win, lon_win, HEADS, inside, head_dim
        )

    scores = product(
        "abhqc,abhkc->abhqk", to_windows(query_heads), to_windows(key_heads)
    ) * head_dim ** (-0.5)
    row_index = jnp.arange(lat_count, dtype=jnp.int32).reshape(lat_win, W_LAT)
    region = (row_index >= lat_count - W_LAT // 2).astype(jnp.int32)
    region_tok = jnp.broadcast_to(region[:, :, None, None], (lat_win, W_LAT, W_LON, LATL)).reshape(
        lat_win, inside
    )
    allowed = (region_tok[:, :, None] == region_tok[:, None, :]).astype(jnp.float32)
    weights = jnp.exp(scores) * allowed[:, None, None, :, :]
    weights = (weights / jnp.sum(weights, axis=-1, keepdims=True)).astype(jnp.bfloat16)
    win_mix = product("abhqk,abhkc->abhqc", weights, to_windows(value_heads)).astype(jnp.bfloat16)
    win_mix = win_mix.reshape(lat_win, lon_win, HEADS, W_LAT, W_LON, LATL, head_dim)
    win_mix = win_mix.transpose(0, 3, 1, 4, 5, 2, 6).reshape(-1, D)
    attended = flat_tokens.astype(jnp.float32) + jnp.dot(
        win_mix, attn_proj, preferred_element_type=jnp.float32
    )
    return attended.astype(jnp.bfloat16).reshape(shifted.shape)


def mlp_block(restored, mlp_gain, mlp_up, mlp_down):
    flat_tokens = restored.reshape(-1, D)
    normed = layer_norm(flat_tokens.astype(jnp.float32), mlp_gain).astype(jnp.bfloat16)
    hidden = jax.nn.gelu(jnp.dot(normed, mlp_up, preferred_element_type=jnp.float32)).astype(
        jnp.bfloat16
    )
    result = flat_tokens.astype(jnp.float32) + jnp.dot(
        hidden, mlp_down, preferred_element_type=jnp.float32
    )
    return result.astype(jnp.bfloat16).reshape(restored.shape)


def shards(
    fields,
    level_ids,
    embed_weight,
    level_embed,
    enc_gain,
    latent_query,
    kv_weight,
    pool_out,
    attn_gain,
    qkv_weight,
    attn_proj,
    mlp_gain,
    mlp_up,
    mlp_down,
    level_mix,
    dec_gain,
    dec_weight,
):
    embeds, mixing = level_tables(level_ids, level_embed, level_mix)
    queries = unit_heads(latent_query.astype(jnp.float32)).astype(jnp.bfloat16)
    query_table, spreader = head_tables(queries)
    field_width = fields.shape[2]
    local_count = fields.shape[1]
    devices = lax.axis_size("lon")
    piece_cols = local_count // devices
    lat_count = devices // ROW_PARTS
    lon_dev = piece_cols * ROW_PARTS
    half_cols = W_LON // 2
    lag = half_cols // piece_cols
    piece = lax.axis_index("lon") // lat_count
    carry = (piece - lag) // ROW_PARTS
    latent_width = LATL * D
    current = fields
    for turn_index in range(STEPS):
        latents = encode(
            current.reshape(local_count, field_width),
            embeds,
            query_table,
            spreader,
            embed_weight,
            enc_gain,
            kv_weight,
            pool_out,
            latent_query,
        )
        blocks = latents.reshape(devices, piece_cols, latent_width)
        blocks = jnp.roll(blocks, carry, axis=0)
        got = lax.all_to_all(
            blocks.reshape(1, local_count, latent_width),
            "lon",
            split_axis=1,
            concat_axis=0,
            tiled=True,
        )
        tiles = got.reshape(ROW_PARTS, lat_count, piece_cols, latent_width).transpose(1, 0, 2, 3)
        tiles = jnp.roll(tiles, -lag, axis=1).reshape(lat_count, lon_dev, latent_width)
        tiles = jnp.roll(tiles, -(W_LAT // 2), axis=0).reshape(lat_count, lon_dev, LATL, D)
        attended = window_block(tiles, attn_gain, qkv_weight, attn_proj)
        backbone_out = mlp_block(attended, mlp_gain, mlp_up, mlp_down)
        values = backbone_out.reshape(lat_count, lon_dev, latent_width)
        extent = values.shape[2]
        values = jnp.roll(values, W_LAT // 2, axis=0)
        values = jnp.roll(values.reshape(lat_count, ROW_PARTS, piece_cols, extent), lag, axis=1)
        outgoing = values.transpose(1, 0, 2, 3).reshape(devices, piece_cols, extent)
        received = lax.all_to_all(outgoing, "lon", split_axis=0, concat_axis=1, tiled=True)
        home = received.reshape(devices, piece_cols, received.shape[2])
        home = jnp.roll(home, -carry, axis=0)
        home_latents = home.reshape(local_count, received.shape[2])
        added = increments(
            home_latents.reshape(local_count, LATL, D), embeds, mixing, dec_gain, dec_weight
        )
        added = added.reshape(current.shape)
        current = (current.astype(jnp.float32) + added.astype(jnp.float32)).astype(jnp.bfloat16)
    return current


def solution(mesh):
    placed = (
        P(("groups", "lon"), None, None),
        P("groups"),
        P(),
        P(),
        P(),
        P(),
        P(),
        P(),
        P(),
        P(),
        P(),
        P(),
        P(),
        P(),
        P(),
        P(),
        P(),
    )
    return jax.shard_map(
        shards,
        mesh=mesh,
        in_specs=placed,
        out_specs=P(("groups", "lon"), None, None),
        check_vma=False,
    )
```

profile of v0, /device:TPU:0, one launch (start us, length us, event | category | flops | bytes accessed | tf_op | source)
XLA Modules:
  0.0 169.1 jit_solution(9471271311963540494)
XLA Ops:
  0.6 1.1 dot_general.83
  2.5 1.3 fusion.138
  5.7 1.2 fusion.142
  7.6 1.8 %copy.290 = f32[96,512]{0,1:T(8,128)} copy(f32[96,512]{1,0:T(8,128)} %slice_multiply_fusion.1) | data formatting | bytes 393216 | tf_op jit(solution)/shard_map/mul | solution.py:32
  9.3 1.0 bitcast_reduce_fusion.1
  11.0 1.8 %copy.291 = f32[96,512]{1,0:T(8,128)} copy(f32[96,512]{0,1:T(8,128)} %bitcast.127) | data formatting | bytes 393216 | tf_op jit(solution)/shard_map/mul | solution.py:33
  13.5 1.3 convert_multiply_fusion
  14.8 1.4 mul.475
  16.1 1.4 reduce_sum.264
  18.8 1.4 mul.477
  21.5 1.7 fusion.17
  23.1 1.4 copy.292
  24.6 1.4 exp.32
  26.0 1.6 exp.31
  30.0 1.0 reshape.615
  31.1 0.9 divide_convert_fusion.5
  32.9 1.2 fusion.8
  35.1 1.0 reduce.8
  36.7 7.4 %all-to-all-start = ((bf16[16,2,1024]{2,1,0:T(2,128)(2,1)}), bf16[16,2,1024]{2,1,0:T(2,128)(2,1)}, u32[]{:S(2)}, u32[]{:S(2)}) async-start(bf16[16,2,1024]{2,1,0:T(2,128)(2,1)} %reshape.632), calls=%async_computation | async-start | bytes 131072 | tf_op jit(solution)/shard_map/all_to_all | solution.py:204
  45.2 1.0 add.248
  47.0 4.1 %all-to-all-done = bf16[16,2,1024]{2,1,0:T(2,128)(2,1)} async-done(((bf16[16,2,1024]{2,1,0:T(2,128)(2,1)}), bf16[16,2,1024]{2,1,0:T(2,128)(2,1)}, u32[]{:S(2)}, u32[]{:S(2)}) %all-to-all-start) | async-done | bytes 65568 | tf_op jit(solution)/shard_map/all_to_all | solution.py:204
  52.0 1.0 bitcast_reduce_fusion.3
  54.8 0.9 reshape.616
  56.0 1.9 %fusion.72 = f32[64,1536]{1,0:T(8,128)S(1)} fusion(bf16[512,1536]{1,0:T(8,128)(2,1)} %param.28, f32[64,512]{1,0:T(8,128)S(1)} %reshape.616, f32[512]{0:T(512)} %param.27, f32[64]{0:T(128)S(1)} %add_rsqrt_fusion.14, f32[64]{0:T(128)S(1)} %broadcast_multiply_fusion.7), kind=kOutput, calls=%fused_computation.140 | convolution fusion | flops 100794368 | bytes 2099712 | tf_op jit(solution)/shard_map/dot_general | solution.py:113
  59.4 1.7 %mul.492 = f32[64,8,64]{2,1,0:T(8,128)} reshape(f32[64,512]{1,0:T(8,128)} %get-tuple-element.13) | data formatting | bytes 262144 | tf_op jit(solution)/shard_map/mul | solution.py:32
  61.1 1.1 reduce_sum.269
  62.8 1.3 add_rsqrt_fusion.4
  65.7 1.7 %mul.494 = f32[64,512]{1,0:T(8,128)} reshape(f32[64,8,64]{2,1,0:T(8,128)} %mul.493) | data formatting | bytes 262144 | tf_op jit(solution)/shard_map/mul | solution.py:33
  67.4 1.7 %mul.497 = f32[64,8,64]{2,1,0:T(8,128)} reshape(f32[64,512]{1,0:T(8,128)} %get-tuple-element.12) | data formatting | bytes 262144 | tf_op jit(solution)/shard_map/mul | solution.py:32
  69.1 1.1 reduce_sum.270
  70.8 1.3 add_rsqrt_fusion.3
  73.7 1.7 %mul.499 = f32[64,512]{1,0:T(8,128)} reshape(f32[64,8,64]{2,1,0:T(8,128)} %mul.498) | data formatting | bytes 262144 | tf_op jit(solution)/shard_map/mul | solution.py:33
  75.4 1.8 %multiply_convert_fusion.11 = (bf16[64,512]{1,0:T(8,128)(2,1)}, bf16[64,512]{1,0:T(8,128)(2,1)}) fusion(f32[64,512]{1,0:T(8,128)} %mul.499, f32[64,1536]{1,0:T(8,128)} %copy-done.2, f32[64,512]{1,0:T(8,128)} %mul.494), kind=kLoop, calls=%fused_computation.112 | loop fusion | flops 131072 | bytes 655360 | tf_op jit(solution)/shard_map/convert_element_type | solution.py:115
  77.2 1.6 reshape.593
  78.8 1.7 copy.306
  80.5 1.6 reshape.595
  82.1 1.7 copy.309
  83.8 1.6 reshape.597
  85.4 1.7 copy.310
  87.0 1.9 %fusion.5 = f32[8,64,64]{1,2,0:T(8,128)} fusion(bf16[8,64,64]{2,1,0:T(8,128)(2,1)} %bitcast.136, bf16[8,64,64]{2,1,0:T(8,128)(2,1)} %bitcast.138, f32[64,64]{0,1:T(8,128)S(1)} %compare_convert_fusion), kind=kOutput, calls=%fused_computation.9 | convolution fusion | flops 4259840 | bytes 278528 | tf_op jit(solution)/shard_map/abhqc,abhkc->abhqk/dot_general | solution.py:20
  88.9 2.0 %convolution_convert_fusion.1 = bf16[8,64,64]{2,1,0:T(8,128)(2,1)} fusion(bf16[8,64,64]{2,1,0:T(8,128)(2,1)} %bitcast.153, f32[8,64,64]{1,2,0:T(8,128)} %fusion.5), kind=kOutput, calls=%fused_computation.13 | convolution fusion | flops 4293183 | bytes 262144 | tf_op jit(solution)/shard_map/abhqk,abhkc->abhqc/dot_general | solution.py:20
  90.9 1.7 %copy.396 = bf16[1,1,8,4,8,2,64]{6,2,5,4,3,1,0:T(8,128)(2,1)} copy(bf16[1,1,8,4,8,2,64]{6,5,4,3,2,1,0:T(2,128)(2,1)} %bitcast.154) | data formatting | bytes 131072 | tf_op jit(solution)/shard_map/reshape | solution.py:136
  92.6 1.1 reshape.600
  93.6 1.4 fusion.139
  95.9 2.6 %fusion.11 = bf16[64,512]{1,0:T(8,128)(2,1)S(1)} fusion(f32[64,512]{1,0:T(8,128)} %copy-done.8, bf16[2048,512]{1,0:T(8,128)(2,1)S(1)} %copy-done, bf16[512,2048]{1,0:T(8,128)(2,1)} %param.31, f32[512]{0:T(512)} %param.30, f32[64]{0:T(128)S(1)} %add_rsqrt_fusion.13, f32[64]{0:T(128)S(1)} %broadcast_multiply_fusion.6), kind=kOutput, calls=%fused_computation.27 | convolution fusion | flops 269811712 | bytes 4393472 | tf_op jit(solution)/shard_map/dot_general | solution.py:150
  99.5 3.5 %all-to-all-start.1 = ((bf16[16,2,1024]{2,1,0:T(2,128)(2,1)}), bf16[16,2,1024]{2,1,0:T(2,128)(2,1)S(1)}, u32[]{:S(2)}, u32[]{:S(2)}) async-start(bf16[16,2,1024]{2,1,0:T(2,128)(2,1)} %bitcast.22), calls=%async_computation.1 | async-start | bytes 131072 | tf_op jit(solution)/shard_map/all_to_all | solution.py:221
  104.3 5.5 %all-to-all-done.1 = bf16[16,2,1024]{2,1,0:T(2,128)(2,1)S(1)} async-done(((bf16[16,2,1024]{2,1,0:T(2,128)(2,1)}), bf16[16,2,1024]{2,1,0:T(2,128)(2,1)S(1)}, u32[]{:S(2)}, u32[]{:S(2)}) %all-to-all-start.1) | async-done | bytes 65568 | tf_op jit(solution)/shard_map/all_to_all | solution.py:221
  113.1 1.7 %mul.516 = f32[96,512]{1,0:T(8,128)} reshape(f32[32,3,512]{2,1,0:T(4,128)} %mul.515.clone) | data formatting | bytes 393216 | tf_op jit(solution)/shard_map/mul | solution.py:96
  115.5 1.7 %mul.525 = f32[96,512]{1,0:T(8,128)} reshape(f32[32,3,512]{2,1,0:T(4,128)} %mul.524.clone) | data formatting | bytes 393216 | tf_op jit(solution)/shard_map/mul | solution.py:97
  117.3 2.2 %fusion.6 = f32[96,500]{1,0:T(8,128)} fusion(bf16[512,500]{0,1:T(8,128)(2,1)} %param.35, f32[96,512]{1,0:T(8,128)S(1)} %add.248, f32[96,512]{1,0:T(8,128)} %mul.525, f32[96,512]{1,0:T(8,128)} %mul.516, f32[512]{0:T(512)} %param.34, f32[96]{0:T(128)S(1)} %rsqrt.134, f32[96]{0:T(128)S(1)} %div.166, f32[96]{0:T(128)} %mul.520, f32[96]{0:T(128)} %mul.462), kind=kOutput, calls=%fused_computation.16 | convolution fusion | flops 49641216 | bytes 1297408 | tf_op jit(solution)/shard_map/dot_general | solution.py:100
  119.5 1.0 reshape.619
  120.5 0.9 add_convert_fusion.1
  121.6 1.3 fusion.140
  124.1 1.2 fusion.143
  127.8 0.9 divide_convert_fusion.4
  130.9 1.0 reduce.9
  131.9 9.7 %all_to_all.16 = bf16[16,2,1024]{2,1,0:T(2,128)(2,1)S(1)} all-to-all(bf16[16,2,1024]{2,1,0:T(2,128)(2,1)S(1)} %reshape.634), channel_id=1, replica_groups=mesh['groups'=2,'lon'=16] {'lon'}, dimensions={0} | all-to-all | bytes 131072 | tf_op jit(solution)/shard_map/all_to_all | solution.py:204
  142.6 1.8 %fusion.74 = f32[64,1536]{1,0:T(8,128)S(1)} fusion(bf16[512,1536]{1,0:T(8,128)(2,1)} %param.28, f32[64,512]{1,0:T(8,128)S(1)} %reshape.621, f32[64]{0:T(128)S(1)} %add_rsqrt_fusion.12, f32[64]{0:T(128)S(1)} %broadcast_multiply_fusion.5, f32[512]{0:T(512)S(1)} %copy-done.20), kind=kOutput, calls=%fused_computation.142 | convolution fusion | flops 100794368 | bytes 2099712 | tf_op jit(solution)/shard_map/dot_general | solution.py:113
  147.2 1.0 reshape.606
  148.5 1.0 reshape.610
  150.5 1.2 convolution_convert_fusion
  152.5 2.5 %fusion.15 = bf16[64,512]{1,0:T(8,128)(2,1)S(1)} fusion(f32[64,512]{1,0:T(8,128)S(1)} %get-tuple-element.43, bf16[2048,512]{1,0:T(8,128)(2,1)S(1)} %copy-done, bf16[512,2048]{1,0:T(8,128)(2,1)} %param.31, f32[64]{0:T(128)S(1)} %add_rsqrt_fusion.11, f32[64]{0:T(128)S(1)} %broadcast_multiply_fusion.4, f32[512]{0:T(512)S(1)} %copy-done.21), kind=kOutput, calls=%fused_computation.31 | convolution fusion | flops 269811712 | bytes 4393472 | tf_op jit(solution)/shard_map/dot_general | solution.py:150
  155.4 9.5 %all_to_all.17 = bf16[16,2,1024]{2,1,0:T(2,128)(2,1)S(1)} all-to-all(bf16[16,2,1024]{2,1,0:T(2,128)(2,1)S(1)} %bitcast.151), channel_id=1, replica_groups=mesh['groups'=2,'lon'=16] {'lon'}, dimensions={0} | all-to-all | bytes 131072 | tf_op jit(solution)/shard_map/all_to_all | solution.py:221
  167.1 1.2 fusion.7
  (241 shorter events, 45.1 us)
Async XLA Ops:
  0.0 95.8 %copy-start = (bf16[2048,512]{1,0:T(8,128)(2,1)S(1)}, bf16[2048,512]{1,0:T(8,128)(2,1)}, u32[]{:S(2)}) copy-start(bf16[2048,512]{1,0:T(8,128)(2,1)} %param.32) | copy-start | bytes 6291460
  0.0 5.7 %copy-start.1 = (bf16[512,1024]{1,0:T(8,128)(2,1)S(1)}, bf16[512,1024]{1,0:T(8,128)(2,1)}, u32[]{:S(2)}) copy-start(bf16[512,1024]{1,0:T(8,128)(2,1)} %param.25) | copy-start | bytes 3145732
  20.9 0.6 copy-start.18
  28.2 18.0 %copy-start.26 = (f32[3,2]{0,1:T(2,128)S(1)}, f32[3,2]{0,1:T(2,128)}, u32[]{:S(2)}) copy-start(f32[3,2]{0,1:T(2,128)} %param.33) | copy-start | bytes 76
  28.2 18.0 %copy-start.27 = (s32[3]{0:T(128)S(1)}, s32[3]{0:T(128)}, u32[]{:S(2)}) copy-start(s32[3]{0:T(128)} %param.20) | copy-start | bytes 40
  28.9 15.5 %copy-start.13 = (f32[2,512]{1,0:T(2,128)}, f32[2,512]{1,0:T(2,128)S(1)}, u32[]{:S(2)}) copy-start(f32[2,512]{1,0:T(2,128)S(1)} %convert_element_type.247) | copy-start | bytes 12292
  36.7 14.4 %all-to-all-start = ((bf16[16,2,1024]{2,1,0:T(2,128)(2,1)}), bf16[16,2,1024]{2,1,0:T(2,128)(2,1)}, u32[]{:S(2)}, u32[]{:S(2)}) async-start(bf16[16,2,1024]{2,1,0:T(2,128)(2,1)} %reshape.632), calls=%async_computation | async-start | bytes 131072 | tf_op jit(solution)/shard_map/all_to_all | solution.py:204
  44.4 42.6 %copy-start.11 = (f32[64,64]{0,1:T(8,128)}, f32[64,64]{0,1:T(8,128)S(1)}, u32[]{:S(2)}) copy-start(f32[64,64]{0,1:T(8,128)S(1)} %compare_convert_fusion) | copy-start | bytes 49156
  46.3 71.0 %copy-start.6 = (f32[96,512]{1,0:T(8,128)}, f32[96,512]{1,0:T(8,128)S(1)}, u32[]{:S(2)}) copy-start(f32[96,512]{1,0:T(8,128)S(1)} %add.248) | copy-start | bytes 589828
  57.9 0.8 copy-start.2
  95.0 0.6 copy-start.8
  95.8 7.1 %copy-start.25 = (f32[3,2]{0,1:T(2,128)S(1)}, f32[3,2]{0,1:T(2,128)}, u32[]{:S(2)}) copy-start(f32[3,2]{0,1:T(2,128)} %fusion.118) | copy-start | bytes 76
  99.5 10.4 %all-to-all-start.1 = ((bf16[16,2,1024]{2,1,0:T(2,128)(2,1)}), bf16[16,2,1024]{2,1,0:T(2,128)(2,1)S(1)}, u32[]{:S(2)}, u32[]{:S(2)}) async-start(bf16[16,2,1024]{2,1,0:T(2,128)(2,1)} %bitcast.22), calls=%async_computation.1 | async-start | bytes 131072 | tf_op jit(solution)/shard_map/all_to_all | solution.py:221
  103.0 6.8 %copy-start.14 = (f32[3]{0:T(128)}, f32[3]{0:T(128)S(1)}, u32[]{:S(2)}) copy-start(f32[3]{0:T(128)S(1)} %get-tuple-element.34) | copy-start | bytes 40
  103.0 6.8 %copy-start.16 = (f32[3]{0:T(128)}, f32[3]{0:T(128)S(1)}, u32[]{:S(2)}) copy-start(f32[3]{0:T(128)S(1)} %get-tuple-element.35) | copy-start | bytes 40
  114.8 8.4 %copy-start.19 = (f32[512]{0:T(512)S(1)}, f32[512]{0:T(512)}, u32[]{:S(2)}) copy-start(f32[512]{0:T(512)} %param.23) | copy-start | bytes 6148
  121.4 1.9 %copy-start.9 = (bf16[1,32,1500]{2,1,0:T(8,128)(2,1)}, bf16[1,32,1500]{2,1,0:T(8,128)(2,1)S(1)}, u32[]{:S(2)}) copy-start(bf16[1,32,1500]{2,1,0:T(8,128)(2,1)S(1)} %add_convert_fusion.1) | copy-start | bytes 288004
  125.3 4.3 %copy-start.3 = (bf16[512,512]{1,0:T(8,128)(2,1)S(1)}, bf16[512,512]{1,0:T(8,128)(2,1)}, u32[]{:S(2)}) copy-start(bf16[512,512]{1,0:T(8,128)(2,1)} %param.26) | copy-start | bytes 1572868
  127.8 14.9 %copy-start.20 = (f32[512]{0:T(512)S(1)}, f32[512]{0:T(512)}, u32[]{:S(2)}) copy-start(f32[512]{0:T(512)} %param.27) | copy-start | bytes 6148
  145.6 4.7 %copy-start.12 = (f32[64,64]{0,1:T(8,128)S(1)}, f32[64,64]{0,1:T(8,128)}, u32[]{:S(2)}) copy-start(f32[64,64]{0,1:T(8,128)} %copy-done.11) | copy-start | bytes 49156
  146.5 5.4 %copy-start.4 = (bf16[512,512]{1,0:T(8,128)(2,1)S(1)}, bf16[512,512]{1,0:T(8,128)(2,1)}, u32[]{:S(2)}) copy-start(bf16[512,512]{1,0:T(8,128)(2,1)} %param.29) | copy-start | bytes 1572868
  148.1 4.3 %copy-start.21 = (f32[512]{0:T(512)S(1)}, f32[512]{0:T(512)}, u32[]{:S(2)}) copy-start(f32[512]{0:T(512)} %param.30) | copy-start | bytes 6148
  152.5 12.8 %copy-start.15 = (f32[3]{0:T(128)S(1)}, f32[3]{0:T(128)}, u32[]{:S(2)}) copy-start(f32[3]{0:T(128)} %copy-done.14) | copy-start | bytes 40
  152.5 12.8 %copy-start.17 = (f32[3]{0:T(128)S(1)}, f32[3]{0:T(128)}, u32[]{:S(2)}) copy-start(f32[3]{0:T(128)} %copy-done.16) | copy-start | bytes 40
  155.0 12.1 %copy-start.5 = (bf16[512,500]{0,1:T(8,128)(2,1)S(1)}, bf16[512,500]{0,1:T(8,128)(2,1)}, u32[]{:S(2)}) copy-start(bf16[512,500]{0,1:T(8,128)(2,1)} %param.35) | copy-start | bytes 1536004
  155.0 12.1 %copy-start.7 = (f32[96,512]{1,0:T(8,128)S(1)}, f32[96,512]{1,0:T(8,128)}, u32[]{:S(2)}) copy-start(f32[96,512]{1,0:T(8,128)} %copy-done.6) | copy-start | bytes 589828
  155.0 12.1 %copy-start.22 = (f32[512]{0:T(512)S(1)}, f32[512]{0:T(512)}, u32[]{:S(2)}) copy-start(f32[512]{0:T(512)} %param.34) | copy-start | bytes 6148
  155.0 12.1 %copy-start.23 = (f32[96]{0:T(128)S(1)}, f32[96]{0:T(128)}, u32[]{:S(2)}) copy-start(f32[96]{0:T(128)} %mul.462) | copy-start | bytes 1156
  155.1 12.0 %copy-start.24 = (f32[96]{0:T(128)S(1)}, f32[96]{0:T(128)}, u32[]{:S(2)}) copy-start(f32[96]{0:T(128)} %mul.520) | copy-start | bytes 1156
  165.1 3.3 %copy-start.10 = (bf16[1,32,1500]{2,1,0:T(8,128)(2,1)S(1)}, bf16[1,32,1500]{2,1,0:T(8,128)(2,1)}, u32[]{:S(2)}) copy-start(bf16[1,32,1500]{2,1,0:T(8,128)(2,1)} %copy-done.9) | copy-start | bytes 288004
where the time goes:
time: 172 us; the launch traced here: 169 us
  local copies, waits for them, and re-layouts  66.6 us (39%)
  matrix products  32.2 us (19%)
  other arithmetic  29.3 us (17%)
  blocking collectives  19.1 us (11%)
  starting transfers between devices  10.9 us (6%)
  waiting for transfers between devices  9.6 us (6%)
    mul x14, local copies, waits for them, and re-layouts, unit_heads(): return (shaped * lax.rsqrt(mean_square + head_eps)).reshape(values.shape)  10.2 us
    all_to_all x1, blocking collectives, shards(): lax.all_to_all(blocks.reshape(1, local_count, latent_width), 'lon', split...  9.66 us
    all_to_all x1, blocking collectives, shards(): lax.all_to_all(outgoing, 'lon', split_axis=0, concat_axis=1, tiled=True)  9.48 us
    all_to_all x1, starting transfers between devices, shards(): lax.all_to_all(blocks.reshape(1, local_count, latent_width), 'lon', split...  7.44 us
    reshape x6, local copies, waits for them, and re-layouts, to_windows(): head_data.reshape(lat_win, W_LAT, lon_win, W_LON, LATL, HEADS, head_dim)  6.95 us
    mul x7, local copies, waits for them, and re-layouts, unit_heads(): mean_square = jnp.mean(shaped * shaped, axis=-1, keepdims=True)  6.84 us
    transpose x6, local copies, waits for them, and re-layouts, to_windows(): shaped.transpose(0, 2, 5, 1, 3, 4, 6)  5.92 us
    all_to_all x1, waiting for transfers between devices, shards(): lax.all_to_all(outgoing, 'lon', split_axis=0, concat_axis=1, tiled=True)  5.53 us
  transfers between devices with their start and end apart: 2, of which 2 were waited for; matrix products, arithmetic and copies ran while one was open for 2% of the time, Pallas kernels for 0%

commit v1 on v0

--- a/solution.py
+++ b/solution.py
@@ -1,3 +1,4 @@
+import functools
 import jax
 import jax.numpy as jnp
 from jax import lax
@@ -14,6 +15,25 @@
 ROW_PARTS = 4
 norm_eps = 1e-05
 head_eps = 1e-06
+
+
+def take_indices_here(my_tile, which_axis):
+    b_next, t_next = (lax.psum(1, which_axis), lax.axis_index(which_axis))
+    local_now = my_tile.shape[0] // b_next
+    s_next = list(my_tile.shape)
+    s_next[0] = local_now
+    x_now = s_next[1]
+    s_next[1] = x_now * b_next
+    w1 = jnp.zeros(s_next, my_tile.dtype)
+    for dev in range(b_next):
+        out_arr = lax.dynamic_slice_in_dim(my_tile, (t_next ^ dev) * local_now, local_now, axis=0)
+        if dev:
+            out_arr = lax.ppermute(out_arr, which_axis, [(dd, dd ^ dev) for dd in range(b_next)])
+        w1 = lax.dynamic_update_slice_in_dim(w1, out_arr, (t_next ^ dev) * x_now, axis=1)
+    return w1
+
+
+build_slices_by_axis = functools.partial(take_indices_here, which_axis="lon")
 
 
 def product(einsum_form, left_side, right_side):
@@ -218,7 +238,7 @@
         values = jnp.roll(values, W_LAT // 2, axis=0)
         values = jnp.roll(values.reshape(lat_count, ROW_PARTS, piece_cols, extent), lag, axis=1)
         outgoing = values.transpose(1, 0, 2, 3).reshape(devices, piece_cols, extent)
-        received = lax.all_to_all(outgoing, "lon", split_axis=0, concat_axis=1, tiled=True)
+        received = build_slices_by_axis(outgoing)
         home = received.reshape(devices, piece_cols, received.shape[2])
         home = jnp.roll(home, -carry, axis=0)
         home_latents = home.reshape(local_count, received.shape[2])

time: 172 us -> 187 us (1.087)
  starting transfers between devices: 10.9 us -> 49.4 us
  local copies, waits for them, and re-layouts: 66.6 us -> 54.7 us
  blocking collectives: 19.1 us -> 12.2 us
  other arithmetic: 29.3 us -> 26.7 us
    ppermute x0 -> x30, starting transfers between devices: none -> 42.1 us  [take_indices_here(): lax.ppermute(out_arr, which_axis, [(dd, dd ^ dev) for dd in range(b_next)])]
    all_to_all x1 -> x0, blocking collectives: 9.48 us -> none  [shards(): lax.all_to_all(outgoing, 'lon', split_axis=0, concat_axis=1, tiled=True)]
    all_to_all x1 -> x0, waiting for transfers between devices: 5.53 us -> none  [shards(): lax.all_to_all(outgoing, 'lon', split_axis=0, concat_axis=1, tiled=True)]
    ppermute x0 -> x30, waiting for transfers between devices: none -> 3.75 us  [take_indices_here(): lax.ppermute(out_arr, which_axis, [(dd, dd ^ dev) for dd in range(b_next)])]
    all_to_all x1 -> x0, starting transfers between devices: 3.5 us -> none  [shards(): lax.all_to_all(outgoing, 'lon', split_axis=0, concat_axis=1, tiled=True)]
    rsqrt x7, other arithmetic: 3.25 us -> 0.73 us  [unit_heads(): return (shaped * lax.rsqrt(mean_square + head_eps)).reshape(values.shape)]
    all_to_all x1, blocking collectives: 9.66 us -> 12.2 us  [shards(): lax.all_to_all(blocks.reshape(1, local_count, latent_width), 'lon', split...]
    transpose x6, local copies, waits for them, and re-layouts: 5.92 us -> 3.72 us  [to_windows(): shaped.transpose(0, 2, 5, 1, 3, 4, 6)]
  transfers between devices with their start and end apart: 2 -> 31, of which waited for: 2 -> 5; matrix products, arithmetic and copies ran while one was open for 2% -> 3% of each run, Pallas kernels for 0% -> 0%
where the time goes in v1:
time: 187 us; the launch traced here: 184 us
  local copies, waits for them, and re-layouts  54.7 us (29%)
  starting transfers between devices  49.4 us (26%)
  matrix products  30.6 us (16%)
  other arithmetic  26.7 us (14%)
  blocking collectives  12.2 us (7%)
  waiting for transfers between devices  8.93 us (5%)
    ppermute x30, starting transfers between devices, take_indices_here(): lax.ppermute(out_arr, which_axis, [(dd, dd ^ dev) for dd in range(b_next)])  42.1 us
    all_to_all x1, blocking collectives, shards(): lax.all_to_all(blocks.reshape(1, local_count, latent_width), 'lon', split...  12.2 us
    mul x14, local copies, waits for them, and re-layouts, unit_heads(): return (shaped * lax.rsqrt(mean_square + head_eps)).reshape(values.shape)  8.44 us
    all_to_all x1, starting transfers between devices, shards(): lax.all_to_all(blocks.reshape(1, local_count, latent_width), 'lon', split...  7.39 us
    reshape x6, local copies, waits for them, and re-layouts, to_windows(): head_data.reshape(lat_win, W_LAT, lon_win, W_LON, LATL, HEADS, head_dim)  5.45 us
    mul x7, local copies, waits for them, and re-layouts, unit_heads(): mean_square = jnp.mean(shaped * shaped, axis=-1, keepdims=True)  5.44 us
    exp x6, local copies, waits for them, and re-layouts, encode(): weights = jnp.exp(scores)  5.27 us
    all_to_all x1, waiting for transfers between devices, shards(): lax.all_to_all(blocks.reshape(1, local_count, latent_width), 'lon', split...  5.18 us
  transfers between devices with their start and end apart: 31, of which 5 were waited for; matrix products, arithmetic and copies ran while one was open for 3% of the time, Pallas kernels for 0%

profile of v1, /device:TPU:0, one launch (start us, length us, event | category | flops | bytes accessed | tf_op | source)
XLA Modules:
  0.0 184.4 jit_solution(11444246375895191884)
XLA Ops:
  0.6 1.1 dot_general.83
  2.5 1.3 fusion.138
  5.7 1.2 fusion.142
  7.6 1.8 copy.290
  9.4 1.0 bitcast_reduce_fusion.1
  11.1 1.8 copy.291
  13.5 1.3 convert_multiply_fusion
  14.8 1.4 mul.539
  16.1 1.4 reduce_sum.264
  18.9 1.4 mul.541
  21.5 1.7 fusion.17
  23.2 1.4 copy.292
  24.6 1.4 exp.32
  26.0 1.6 exp.31
  30.0 1.0 reshape.613
  31.1 0.9 divide_convert_fusion.5
  33.0 1.2 fusion.8
  35.2 1.0 reduce.8
  36.8 7.4 %all-to-all-start = ((bf16[16,2,1024]{2,1,0:T(2,128)(2,1)}), bf16[16,2,1024]{2,1,0:T(2,128)(2,1)S(1)}, u32[]{:S(2)}, u32[]{:S(2)}) async-start(bf16[16,2,1024]{2,1,0:T(2,128)(2,1)} %reshape.630), calls=%async_computation | async-start | bytes 131072 | tf_op jit(solution)/shard_map/all_to_all | solution.py:224
  45.9 5.2 %all-to-all-done = bf16[16,2,1024]{2,1,0:T(2,128)(2,1)S(1)} async-done(((bf16[16,2,1024]{2,1,0:T(2,128)(2,1)}), bf16[16,2,1024]{2,1,0:T(2,128)(2,1)S(1)}, u32[]{:S(2)}, u32[]{:S(2)}) %all-to-all-start) | async-done | bytes 65568 | tf_op jit(solution)/shard_map/all_to_all | solution.py:224
  52.2 1.8 fusion.72
  55.5 1.0 mul.556
  60.5 1.0 mul.561
  65.4 1.7 multiply_convert_fusion.11
  67.4 1.6 reshape.591
  69.0 1.0 copy.309
  70.0 1.6 reshape.593
  71.6 1.7 copy.310
  73.3 1.7 fusion.5
  75.0 1.3 convolution_convert_fusion.1
  76.6 1.4 fusion.139
  78.2 2.6 %fusion.11 = bf16[64,512]{1,0:T(8,128)(2,1)S(1)} fusion(f32[64,512]{1,0:T(8,128)S(1)} %get-tuple-element.71, bf16[2048,512]{1,0:T(8,128)(2,1)S(1)} %copy-done, bf16[512,2048]{1,0:T(8,128)(2,1)} %param.31, f32[512]{0:T(512)} %param.30, f32[64]{0:T(128)S(1)} %add_rsqrt_fusion.13, f32[64]{0:T(128)S(1)} %broadcast_multiply_fusion.6), kind=kOutput, calls=%fused_computation.27 | convolution fusion | flops 269811712 | bytes 4393472 | tf_op jit(solution)/shard_map/dot_general | solution.py:170
  82.2 1.0 add.408
  84.7 1.6 collective-permute-start.2
  86.4 1.7 collective-permute-start.4
  88.3 2.4 %collective-permute-start.6 = (bf16[1,2,1024]{2,1,0:T(2,128)(2,1)S(1)}, bf16[1,2,1024]{2,1,0:T(2,128)(2,1)S(1)}, u32[]{:S(2)}, u32[]{:S(2)}) collective-permute-start(bf16[1,2,1024]{2,1,0:T(2,128)(2,1)S(1)} %get-tuple-element.50), channel_id=1, source_target_pairs={{0,7},{1,6},{2,5},{3,4},{4,3},{5,2},{6,1},{7,0},{8,15},{9,14},{10,... | collective-permute-start | bytes 12296 | tf_op jit(solution)/shard_map/ppermute | solution.py:31
  91.1 2.5 %collective-permute-start.8 = (bf16[1,2,1024]{2,1,0:T(2,128)(2,1)S(1)}, bf16[1,2,1024]{2,1,0:T(2,128)(2,1)S(1)}, u32[]{:S(2)}, u32[]{:S(2)}) collective-permute-start(bf16[1,2,1024]{2,1,0:T(2,128)(2,1)S(1)} %get-tuple-element.48), channel_id=1, source_target_pairs={{0,9},{1,8},{2,11},{3,10},{4,13},{5,12},{6,15},{7,14},{8,1},{9,0},... | collective-permute-start | bytes 12296 | tf_op jit(solution)/shard_map/ppermute | solution.py:31
  94.1 3.3 %collective-permute-start.10 = (bf16[1,2,1024]{2,1,0:T(2,128)(2,1)S(1)}, bf16[1,2,1024]{2,1,0:T(2,128)(2,1)S(1)}, u32[]{:S(2)}, u32[]{:S(2)}) collective-permute-start(bf16[1,2,1024]{2,1,0:T(2,128)(2,1)S(1)} %get-tuple-element.46), channel_id=1, source_target_pairs={{0,11},{1,10},{2,9},{3,8},{4,15},{5,14},{6,13},{7,12},{8,3},{9,2},... | collective-permute-start | bytes 12296 | tf_op jit(solution)/shard_map/ppermute | solution.py:31
  98.0 3.1 %collective-permute-start.12 = (bf16[1,2,1024]{2,1,0:T(2,128)(2,1)S(1)}, bf16[1,2,1024]{2,1,0:T(2,128)(2,1)S(1)}, u32[]{:S(2)}, u32[]{:S(2)}) collective-permute-start(bf16[1,2,1024]{2,1,0:T(2,128)(2,1)S(1)} %get-tuple-element.44), channel_id=1, source_target_pairs={{0,13},{1,12},{2,15},{3,14},{4,9},{5,8},{6,11},{7,10},{8,5},{9,4},... | collective-permute-start | bytes 12296 | tf_op jit(solution)/shard_map/ppermute | solution.py:31
  101.8 3.8 %collective-permute-start.14 = (bf16[1,2,1024]{2,1,0:T(2,128)(2,1)S(1)}, bf16[1,2,1024]{2,1,0:T(2,128)(2,1)S(1)}, u32[]{:S(2)}, u32[]{:S(2)}) collective-permute-start(bf16[1,2,1024]{2,1,0:T(2,128)(2,1)S(1)} %get-tuple-element.42), channel_id=1, source_target_pairs={{0,15},{1,14},{2,13},{3,12},{4,11},{5,10},{6,9},{7,8},{8,7},{9,6},... | collective-permute-start | bytes 12296 | tf_op jit(solution)/shard_map/ppermute | solution.py:31
  105.8 1.7 collective-permute-done.13
  111.9 1.7 mul.596
  114.3 1.0 mul.605
  115.4 2.2 %fusion.6 = f32[96,500]{1,0:T(8,128)} fusion(bf16[512,500]{0,1:T(8,128)(2,1)} %param.35, f32[96,512]{1,0:T(8,128)S(1)} %add.408, f32[96,512]{1,0:T(8,128)S(1)} %mul.605, f32[96,512]{1,0:T(8,128)} %mul.596, f32[512]{0:T(512)} %param.34, f32[96]{0:T(128)} %rsqrt.134, f32[96]{0:T(128)} %div.166, f32[96]{0:T(128)} %mul.600, f32[96]{0:T(128)} %mul.526), kind=kOutput, calls=%fused_computation.16 | convolution fusion | flops 49641216 | bytes 1297408 | tf_op jit(solution)/shard_map/dot_general | solution.py:120
  117.5 1.0 reshape.617
  119.7 1.3 fusion.140
  122.8 1.2 fusion.143
  126.5 0.9 divide_convert_fusion.4
  129.6 1.0 reduce.9
  130.6 12.2 %all_to_all.8 = bf16[16,2,1024]{2,1,0:T(2,128)(2,1)S(1)} all-to-all(bf16[16,2,1024]{2,1,0:T(2,128)(2,1)S(1)} %reshape.632), channel_id=1, replica_groups=mesh['groups'=2,'lon'=16] {'lon'}, dimensions={0} | all-to-all | bytes 131072 | tf_op jit(solution)/shard_map/all_to_all | solution.py:224
  143.9 1.8 fusion.74
  148.4 1.0 reshape.603
  149.8 1.0 reshape.607
  151.7 1.2 convolution_convert_fusion
  153.7 2.5 %fusion.15 = bf16[64,512]{1,0:T(8,128)(2,1)S(1)} fusion(f32[64,512]{1,0:T(8,128)S(1)} %get-tuple-element.75, bf16[2048,512]{1,0:T(8,128)(2,1)S(1)} %copy-done, bf16[512,2048]{1,0:T(8,128)(2,1)} %param.31, f32[64]{0:T(128)S(1)} %add_rsqrt_fusion.11, f32[64]{0:T(128)S(1)} %broadcast_multiply_fusion.4, f32[512]{0:T(512)S(1)} %copy-done.19), kind=kOutput, calls=%fused_computation.31 | convolution fusion | flops 269811712 | bytes 4393472 | tf_op jit(solution)/shard_map/dot_general | solution.py:170
  157.1 1.6 collective-permute-start.17
  158.9 1.5 collective-permute-start.19
  160.7 2.5 %collective-permute-start.21 = (bf16[1,2,1024]{2,1,0:T(2,128)(2,1)S(1)}, bf16[1,2,1024]{2,1,0:T(2,128)(2,1)S(1)}, u32[]{:S(2)}, u32[]{:S(2)}) collective-permute-start(bf16[1,2,1024]{2,1,0:T(2,128)(2,1)S(1)} %get-tuple-element.24), channel_id=1, source_target_pairs={{0,7},{1,6},{2,5},{3,4},{4,3},{5,2},{6,1},{7,0},{8,15},{9,14},{10,... | collective-permute-start | bytes 12296 | tf_op jit(solution)/shard_map/ppermute | solution.py:31
  163.6 2.4 %collective-permute-start.23 = (bf16[1,2,1024]{2,1,0:T(2,128)(2,1)S(1)}, bf16[1,2,1024]{2,1,0:T(2,128)(2,1)S(1)}, u32[]{:S(2)}, u32[]{:S(2)}) collective-permute-start(bf16[1,2,1024]{2,1,0:T(2,128)(2,1)S(1)} %get-tuple-element.22), channel_id=1, source_target_pairs={{0,9},{1,8},{2,11},{3,10},{4,13},{5,12},{6,15},{7,14},{8,1},{9,0},... | collective-permute-start | bytes 12296 | tf_op jit(solution)/shard_map/ppermute | solution.py:31
  166.5 3.3 %collective-permute-start.25 = (bf16[1,2,1024]{2,1,0:T(2,128)(2,1)S(1)}, bf16[1,2,1024]{2,1,0:T(2,128)(2,1)S(1)}, u32[]{:S(2)}, u32[]{:S(2)}) collective-permute-start(bf16[1,2,1024]{2,1,0:T(2,128)(2,1)S(1)} %get-tuple-element.20), channel_id=1, source_target_pairs={{0,11},{1,10},{2,9},{3,8},{4,15},{5,14},{6,13},{7,12},{8,3},{9,2},... | collective-permute-start | bytes 12296 | tf_op jit(solution)/shard_map/ppermute | solution.py:31
  170.4 3.0 %collective-permute-start.27 = (bf16[1,2,1024]{2,1,0:T(2,128)(2,1)S(1)}, bf16[1,2,1024]{2,1,0:T(2,128)(2,1)S(1)}, u32[]{:S(2)}, u32[]{:S(2)}) collective-permute-start(bf16[1,2,1024]{2,1,0:T(2,128)(2,1)S(1)} %get-tuple-element.18), channel_id=1, source_target_pairs={{0,13},{1,12},{2,15},{3,14},{4,9},{5,8},{6,11},{7,10},{8,5},{9,4},... | collective-permute-start | bytes 12296 | tf_op jit(solution)/shard_map/ppermute | solution.py:31
  174.3 3.8 %collective-permute-start.29 = (bf16[1,2,1024]{2,1,0:T(2,128)(2,1)S(1)}, bf16[1,2,1024]{2,1,0:T(2,128)(2,1)S(1)}, u32[]{:S(2)}, u32[]{:S(2)}) collective-permute-start(bf16[1,2,1024]{2,1,0:T(2,128)(2,1)S(1)} %get-tuple-element.16), channel_id=1, source_target_pairs={{0,15},{1,14},{2,13},{3,12},{4,11},{5,10},{6,9},{7,8},{8,7},{9,6},... | collective-permute-start | bytes 12296 | tf_op jit(solution)/shard_map/ppermute | solution.py:31
  178.3 1.6 collective-permute-done.28
  182.4 1.2 fusion.7
  (328 shorter events, 55.6 us)
Async XLA Ops:
  0.0 78.2 %copy-start = (bf16[2048,512]{1,0:T(8,128)(2,1)S(1)}, bf16[2048,512]{1,0:T(8,128)(2,1)}, u32[]{:S(2)}) copy-start(bf16[2048,512]{1,0:T(8,128)(2,1)} %param.32) | copy-start | bytes 6291460
  0.0 5.7 %copy-start.1 = (bf16[512,1024]{1,0:T(8,128)(2,1)S(1)}, bf16[512,1024]{1,0:T(8,128)(2,1)}, u32[]{:S(2)}) copy-start(bf16[512,1024]{1,0:T(8,128)(2,1)} %param.25) | copy-start | bytes 3145732
  20.9 0.6 copy-start.16
  28.3 16.9 %copy-start.23 = (f32[3,2]{0,1:T(2,128)S(1)}, f32[3,2]{0,1:T(2,128)}, u32[]{:S(2)}) copy-start(f32[3,2]{0,1:T(2,128)} %param.33) | copy-start | bytes 76
  28.3 16.9 %copy-start.24 = (s32[3]{0:T(128)S(1)}, s32[3]{0:T(128)}, u32[]{:S(2)}) copy-start(s32[3]{0:T(128)} %param.20) | copy-start | bytes 40
  29.0 22.6 %copy-start.11 = (f32[2,512]{1,0:T(2,128)}, f32[2,512]{1,0:T(2,128)S(1)}, u32[]{:S(2)}) copy-start(f32[2,512]{1,0:T(2,128)S(1)} %convert_element_type.247) | copy-start | bytes 12292
  31.1 21.1 %copy-start.17 = (f32[512]{0:T(512)S(1)}, f32[512]{0:T(512)}, u32[]{:S(2)}) copy-start(f32[512]{0:T(512)} %param.27) | copy-start | bytes 6148
  36.8 14.3 %all-to-all-start = ((bf16[16,2,1024]{2,1,0:T(2,128)(2,1)}), bf16[16,2,1024]{2,1,0:T(2,128)(2,1)S(1)}, u32[]{:S(2)}, u32[]{:S(2)}) async-start(bf16[16,2,1024]{2,1,0:T(2,128)(2,1)} %reshape.630), calls=%async_computation | async-start | bytes 131072 | tf_op jit(solution)/shard_map/all_to_all | solution.py:224
  54.1 0.8 copy-start.2
  78.2 5.1 %copy-start.12 = (f32[3]{0:T(128)S(1)}, f32[3]{0:T(128)}, u32[]{:S(2)}) copy-start(f32[3]{0:T(128)} %get-tuple-element.66) | copy-start | bytes 40
  78.2 5.8 %copy-start.14 = (f32[3]{0:T(128)S(1)}, f32[3]{0:T(128)}, u32[]{:S(2)}) copy-start(f32[3]{0:T(128)} %get-tuple-element.67) | copy-start | bytes 40
  81.3 6.8 %collective-permute-start = (bf16[1,2,1024]{2,1,0:T(2,128)(2,1)S(1)}, bf16[1,2,1024]{2,1,0:T(2,128)(2,1)S(1)}, u32[]{:S(2)}, u32[]{:S(2)}) collective-permute-start(bf16[1,2,1024]{2,1,0:T(2,128)(2,1)S(1)} %get-tuple-element.56), channel_id=1, source_target_pairs={{0,1},{1,0},{2,3},{3,2},{4,5},{5,4},{6,7},{7,6},{8,9},{9,8},{10,11... | collective-permute-start | bytes 12296 | tf_op jit(solution)/shard_map/ppermute | solution.py:31
  83.2 34.3 %copy-start.6 = (f32[96,512]{1,0:T(8,128)}, f32[96,512]{1,0:T(8,128)S(1)}, u32[]{:S(2)}) copy-start(f32[96,512]{1,0:T(8,128)S(1)} %add.408) | copy-start | bytes 589828
  84.6 3.8 %collective-permute-start.1 = (bf16[1,2,1024]{2,1,0:T(2,128)(2,1)S(1)}, bf16[1,2,1024]{2,1,0:T(2,128)(2,1)S(1)}, u32[]{:S(2)}, u32[]{:S(2)}) collective-permute-start(bf16[1,2,1024]{2,1,0:T(2,128)(2,1)S(1)} %get-tuple-element.55), channel_id=1, source_target_pairs={{0,2},{1,3},{2,0},{3,1},{4,6},{5,7},{6,4},{7,5},{8,10},{9,11},{10,... | collective-permute-start | bytes 12296 | tf_op jit(solution)/shard_map/ppermute | solution.py:31
  84.7 6.1 %collective-permute-start.2 = (bf16[1,2,1024]{2,1,0:T(2,128)(2,1)S(1)}, bf16[1,2,1024]{2,1,0:T(2,128)(2,1)S(1)}, u32[]{:S(2)}, u32[]{:S(2)}) collective-permute-start(bf16[1,2,1024]{2,1,0:T(2,128)(2,1)S(1)} %get-tuple-element.54), channel_id=1, source_target_pairs={{0,3},{1,2},{2,1},{3,0},{4,7},{5,6},{6,5},{7,4},{8,11},{9,10},{10,... | collective-permute-start | bytes 12296 | tf_op jit(solution)/shard_map/ppermute | solution.py:31
  86.3 4.8 %collective-permute-start.3 = (bf16[1,2,1024]{2,1,0:T(2,128)(2,1)S(1)}, bf16[1,2,1024]{2,1,0:T(2,128)(2,1)S(1)}, u32[]{:S(2)}, u32[]{:S(2)}) collective-permute-start(bf16[1,2,1024]{2,1,0:T(2,128)(2,1)S(1)} %get-tuple-element.53), channel_id=1, source_target_pairs={{0,4},{1,5},{2,6},{3,7},{4,0},{5,1},{6,2},{7,3},{8,12},{9,13},{10,... | collective-permute-start | bytes 12296 | tf_op jit(solution)/shard_map/ppermute | solution.py:31
  86.4 7.2 %collective-permute-start.4 = (bf16[1,2,1024]{2,1,0:T(2,128)(2,1)S(1)}, bf16[1,2,1024]{2,1,0:T(2,128)(2,1)S(1)}, u32[]{:S(2)}, u32[]{:S(2)}) collective-permute-start(bf16[1,2,1024]{2,1,0:T(2,128)(2,1)S(1)} %get-tuple-element.52), channel_id=1, source_target_pairs={{0,5},{1,4},{2,7},{3,6},{4,1},{5,0},{6,3},{7,2},{8,13},{9,12},{10,... | collective-permute-start | bytes 12296 | tf_op jit(solution)/shard_map/ppermute | solution.py:31
  88.1 6.0 %collective-permute-start.5 = (bf16[1,2,1024]{2,1,0:T(2,128)(2,1)S(1)}, bf16[1,2,1024]{2,1,0:T(2,128)(2,1)S(1)}, u32[]{:S(2)}, u32[]{:S(2)}) collective-permute-start(bf16[1,2,1024]{2,1,0:T(2,128)(2,1)S(1)} %get-tuple-element.51), channel_id=1, source_target_pairs={{0,6},{1,7},{2,4},{3,5},{4,2},{5,3},{6,0},{7,1},{8,14},{9,15},{10,... | collective-permute-start | bytes 12296 | tf_op jit(solution)/shard_map/ppermute | solution.py:31
  88.3 9.0 %collective-permute-start.6 = (bf16[1,2,1024]{2,1,0:T(2,128)(2,1)S(1)}, bf16[1,2,1024]{2,1,0:T(2,128)(2,1)S(1)}, u32[]{:S(2)}, u32[]{:S(2)}) collective-permute-start(bf16[1,2,1024]{2,1,0:T(2,128)(2,1)S(1)} %get-tuple-element.50), channel_id=1, source_target_pairs={{0,7},{1,6},{2,5},{3,4},{4,3},{5,2},{6,1},{7,0},{8,15},{9,14},{10,... | collective-permute-start | bytes 12296 | tf_op jit(solution)/shard_map/ppermute | solution.py:31
  90.8 7.2 %collective-permute-start.7 = (bf16[1,2,1024]{2,1,0:T(2,128)(2,1)S(1)}, bf16[1,2,1024]{2,1,0:T(2,128)(2,1)S(1)}, u32[]{:S(2)}, u32[]{:S(2)}) collective-permute-start(bf16[1,2,1024]{2,1,0:T(2,128)(2,1)S(1)} %get-tuple-element.49), channel_id=1, source_target_pairs={{0,8},{1,9},{2,10},{3,11},{4,12},{5,13},{6,14},{7,15},{8,0},{9,1},... | collective-permute-start | bytes 12296 | tf_op jit(solution)/shard_map/ppermute | solution.py:31
  91.1 10.0 %collective-permute-start.8 = (bf16[1,2,1024]{2,1,0:T(2,128)(2,1)S(1)}, bf16[1,2,1024]{2,1,0:T(2,128)(2,1)S(1)}, u32[]{:S(2)}, u32[]{:S(2)}) collective-permute-start(bf16[1,2,1024]{2,1,0:T(2,128)(2,1)S(1)} %get-tuple-element.48), channel_id=1, source_target_pairs={{0,9},{1,8},{2,11},{3,10},{4,13},{5,12},{6,15},{7,14},{8,1},{9,0},... | collective-permute-start | bytes 12296 | tf_op jit(solution)/shard_map/ppermute | solution.py:31
  93.7 8.2 %collective-permute-start.9 = (bf16[1,2,1024]{2,1,0:T(2,128)(2,1)S(1)}, bf16[1,2,1024]{2,1,0:T(2,128)(2,1)S(1)}, u32[]{:S(2)}, u32[]{:S(2)}) collective-permute-start(bf16[1,2,1024]{2,1,0:T(2,128)(2,1)S(1)} %get-tuple-element.47), channel_id=1, source_target_pairs={{0,10},{1,11},{2,8},{3,9},{4,14},{5,15},{6,12},{7,13},{8,2},{9,3},... | collective-permute-start | bytes 12296 | tf_op jit(solution)/shard_map/ppermute | solution.py:31
  94.1 11.6 %collective-permute-start.10 = (bf16[1,2,1024]{2,1,0:T(2,128)(2,1)S(1)}, bf16[1,2,1024]{2,1,0:T(2,128)(2,1)S(1)}, u32[]{:S(2)}, u32[]{:S(2)}) collective-permute-start(bf16[1,2,1024]{2,1,0:T(2,128)(2,1)S(1)} %get-tuple-element.46), channel_id=1, source_target_pairs={{0,11},{1,10},{2,9},{3,8},{4,15},{5,14},{6,13},{7,12},{8,3},{9,2},... | collective-permute-start | bytes 12296 | tf_op jit(solution)/shard_map/ppermute | solution.py:31
  97.3 8.4 %collective-permute-start.11 = (bf16[1,2,1024]{2,1,0:T(2,128)(2,1)S(1)}, bf16[1,2,1024]{2,1,0:T(2,128)(2,1)S(1)}, u32[]{:S(2)}, u32[]{:S(2)}) collective-permute-start(bf16[1,2,1024]{2,1,0:T(2,128)(2,1)S(1)} %get-tuple-element.45), channel_id=1, source_target_pairs={{0,12},{1,13},{2,14},{3,15},{4,8},{5,9},{6,10},{7,11},{8,4},{9,5},... | collective-permute-start | bytes 12296 | tf_op jit(solution)/shard_map/ppermute | solution.py:31
  98.0 7.8 %collective-permute-start.12 = (bf16[1,2,1024]{2,1,0:T(2,128)(2,1)S(1)}, bf16[1,2,1024]{2,1,0:T(2,128)(2,1)S(1)}, u32[]{:S(2)}, u32[]{:S(2)}) collective-permute-start(bf16[1,2,1024]{2,1,0:T(2,128)(2,1)S(1)} %get-tuple-element.44), channel_id=1, source_target_pairs={{0,13},{1,12},{2,15},{3,14},{4,9},{5,8},{6,11},{7,10},{8,5},{9,4},... | collective-permute-start | bytes 12296 | tf_op jit(solution)/shard_map/ppermute | solution.py:31
  101.1 6.4 %collective-permute-start.13 = (bf16[1,2,1024]{2,1,0:T(2,128)(2,1)S(1)}, bf16[1,2,1024]{2,1,0:T(2,128)(2,1)S(1)}, u32[]{:S(2)}, u32[]{:S(2)}) collective-permute-start(bf16[1,2,1024]{2,1,0:T(2,128)(2,1)S(1)} %get-tuple-element.43), channel_id=1, source_target_pairs={{0,14},{1,15},{2,12},{3,13},{4,10},{5,11},{6,8},{7,9},{8,6},{9,7},... | collective-permute-start | bytes 12296 | tf_op jit(solution)/shard_map/ppermute | solution.py:31
  101.8 5.8 %collective-permute-start.14 = (bf16[1,2,1024]{2,1,0:T(2,128)(2,1)S(1)}, bf16[1,2,1024]{2,1,0:T(2,128)(2,1)S(1)}, u32[]{:S(2)}, u32[]{:S(2)}) collective-permute-start(bf16[1,2,1024]{2,1,0:T(2,128)(2,1)S(1)} %get-tuple-element.42), channel_id=1, source_target_pairs={{0,15},{1,14},{2,13},{3,12},{4,11},{5,10},{6,9},{7,8},{8,7},{9,6},... | collective-permute-start | bytes 12296 | tf_op jit(solution)/shard_map/ppermute | solution.py:31
  119.5 2.6 %copy-start.8 = (bf16[1,32,1500]{2,1,0:T(8,128)(2,1)}, bf16[1,32,1500]{2,1,0:T(8,128)(2,1)S(1)}, u32[]{:S(2)}) copy-start(bf16[1,32,1500]{2,1,0:T(8,128)(2,1)S(1)} %add_convert_fusion.1) | copy-start | bytes 288004
  124.1 4.3 %copy-start.3 = (bf16[512,512]{1,0:T(8,128)(2,1)S(1)}, bf16[512,512]{1,0:T(8,128)(2,1)}, u32[]{:S(2)}) copy-start(bf16[512,512]{1,0:T(8,128)(2,1)} %param.26) | copy-start | bytes 1572868
  126.5 17.4 %copy-start.18 = (f32[512]{0:T(512)S(1)}, f32[512]{0:T(512)}, u32[]{:S(2)}) copy-start(f32[512]{0:T(512)} %param.27) | copy-start | bytes 6148
  146.8 4.7 %copy-start.10 = (f32[64,64]{0,1:T(8,128)S(1)}, f32[64,64]{0,1:T(8,128)}, u32[]{:S(2)}) copy-start(f32[64,64]{0,1:T(8,128)} %compare_convert_fusion) | copy-start | bytes 49156
  147.8 5.4 %copy-start.4 = (bf16[512,512]{1,0:T(8,128)(2,1)S(1)}, bf16[512,512]{1,0:T(8,128)(2,1)}, u32[]{:S(2)}) copy-start(bf16[512,512]{1,0:T(8,128)(2,1)} %param.29) | copy-start | bytes 1572868
  149.4 4.3 %copy-start.19 = (f32[512]{0:T(512)S(1)}, f32[512]{0:T(512)}, u32[]{:S(2)}) copy-start(f32[512]{0:T(512)} %param.30) | copy-start | bytes 6148
  153.7 26.8 %copy-start.13 = (f32[3]{0:T(128)S(1)}, f32[3]{0:T(128)}, u32[]{:S(2)}) copy-start(f32[3]{0:T(128)} %get-tuple-element.66) | copy-start | bytes 40
  153.7 26.8 %copy-start.15 = (f32[3]{0:T(128)S(1)}, f32[3]{0:T(128)}, u32[]{:S(2)}) copy-start(f32[3]{0:T(128)} %get-tuple-element.67) | copy-start | bytes 40
  156.3 26.1 %copy-start.5 = (bf16[512,500]{0,1:T(8,128)(2,1)S(1)}, bf16[512,500]{0,1:T(8,128)(2,1)}, u32[]{:S(2)}) copy-start(bf16[512,500]{0,1:T(8,128)(2,1)} %param.35) | copy-start | bytes 1536004
  156.3 26.1 %copy-start.7 = (f32[96,512]{1,0:T(8,128)S(1)}, f32[96,512]{1,0:T(8,128)}, u32[]{:S(2)}) copy-start(f32[96,512]{1,0:T(8,128)} %copy-done.6) | copy-start | bytes 589828
  156.3 26.1 %copy-start.20 = (f32[512]{0:T(512)S(1)}, f32[512]{0:T(512)}, u32[]{:S(2)}) copy-start(f32[512]{0:T(512)} %param.34) | copy-start | bytes 6148
  156.3 26.1 %copy-start.21 = (f32[96]{0:T(128)S(1)}, f32[96]{0:T(128)}, u32[]{:S(2)}) copy-start(f32[96]{0:T(128)} %mul.526) | copy-start | bytes 1156
  156.3 26.0 %copy-start.22 = (f32[96]{0:T(128)S(1)}, f32[96]{0:T(128)}, u32[]{:S(2)}) copy-start(f32[96]{0:T(128)} %mul.600) | copy-start | bytes 1156
  156.8 3.6 %collective-permute-start.15 = (bf16[1,2,1024]{2,1,0:T(2,128)(2,1)S(1)}, bf16[1,2,1024]{2,1,0:T(2,128)(2,1)S(1)}, u32[]{:S(2)}, u32[]{:S(2)}) collective-permute-start(bf16[1,2,1024]{2,1,0:T(2,128)(2,1)S(1)} %get-tuple-element.30), channel_id=1, source_target_pairs={{0,1},{1,0},{2,3},{3,2},{4,5},{5,4},{6,7},{7,6},{8,9},{9,8},{10,11... | collective-permute-start | bytes 12296 | tf_op jit(solution)/shard_map/ppermute | solution.py:31
  156.9 3.8 %collective-permute-start.16 = (bf16[1,2,1024]{2,1,0:T(2,128)(2,1)S(1)}, bf16[1,2,1024]{2,1,0:T(2,128)(2,1)S(1)}, u32[]{:S(2)}, u32[]{:S(2)}) collective-permute-start(bf16[1,2,1024]{2,1,0:T(2,128)(2,1)S(1)} %get-tuple-element.29), channel_id=1, source_target_pairs={{0,2},{1,3},{2,0},{3,1},{4,6},{5,7},{6,4},{7,5},{8,10},{9,11},{10,... | collective-permute-start | bytes 12296 | tf_op jit(solution)/shard_map/ppermute | solution.py:31
  157.1 6.1 %collective-permute-start.17 = (bf16[1,2,1024]{2,1,0:T(2,128)(2,1)S(1)}, bf16[1,2,1024]{2,1,0:T(2,128)(2,1)S(1)}, u32[]{:S(2)}, u32[]{:S(2)}) collective-permute-start(bf16[1,2,1024]{2,1,0:T(2,128)(2,1)S(1)} %get-tuple-element.28), channel_id=1, source_target_pairs={{0,3},{1,2},{2,1},{3,0},{4,7},{5,6},{6,5},{7,4},{8,11},{9,10},{10,... | collective-permute-start | bytes 12296 | tf_op jit(solution)/shard_map/ppermute | solution.py:31
  158.8 4.8 %collective-permute-start.18 = (bf16[1,2,1024]{2,1,0:T(2,128)(2,1)S(1)}, bf16[1,2,1024]{2,1,0:T(2,128)(2,1)S(1)}, u32[]{:S(2)}, u32[]{:S(2)}) collective-permute-start(bf16[1,2,1024]{2,1,0:T(2,128)(2,1)S(1)} %get-tuple-element.27), channel_id=1, source_target_pairs={{0,4},{1,5},{2,6},{3,7},{4,0},{5,1},{6,2},{7,3},{8,12},{9,13},{10,... | collective-permute-start | bytes 12296 | tf_op jit(solution)/shard_map/ppermute | solution.py:31
  158.9 7.1 %collective-permute-start.19 = (bf16[1,2,1024]{2,1,0:T(2,128)(2,1)S(1)}, bf16[1,2,1024]{2,1,0:T(2,128)(2,1)S(1)}, u32[]{:S(2)}, u32[]{:S(2)}) collective-permute-start(bf16[1,2,1024]{2,1,0:T(2,128)(2,1)S(1)} %get-tuple-element.26), channel_id=1, source_target_pairs={{0,5},{1,4},{2,7},{3,6},{4,1},{5,0},{6,3},{7,2},{8,13},{9,12},{10,... | collective-permute-start | bytes 12296 | tf_op jit(solution)/shard_map/ppermute | solution.py:31
  160.5 6.0 %collective-permute-start.20 = (bf16[1,2,1024]{2,1,0:T(2,128)(2,1)S(1)}, bf16[1,2,1024]{2,1,0:T(2,128)(2,1)S(1)}, u32[]{:S(2)}, u32[]{:S(2)}) collective-permute-start(bf16[1,2,1024]{2,1,0:T(2,128)(2,1)S(1)} %get-tuple-element.25), channel_id=1, source_target_pairs={{0,6},{1,7},{2,4},{3,5},{4,2},{5,3},{6,0},{7,1},{8,14},{9,15},{10,... | collective-permute-start | bytes 12296 | tf_op jit(solution)/shard_map/ppermute | solution.py:31
  160.7 9.1 %collective-permute-start.21 = (bf16[1,2,1024]{2,1,0:T(2,128)(2,1)S(1)}, bf16[1,2,1024]{2,1,0:T(2,128)(2,1)S(1)}, u32[]{:S(2)}, u32[]{:S(2)}) collective-permute-start(bf16[1,2,1024]{2,1,0:T(2,128)(2,1)S(1)} %get-tuple-element.24), channel_id=1, source_target_pairs={{0,7},{1,6},{2,5},{3,4},{4,3},{5,2},{6,1},{7,0},{8,15},{9,14},{10,... | collective-permute-start | bytes 12296 | tf_op jit(solution)/shard_map/ppermute | solution.py:31
  163.3 7.1 %collective-permute-start.22 = (bf16[1,2,1024]{2,1,0:T(2,128)(2,1)S(1)}, bf16[1,2,1024]{2,1,0:T(2,128)(2,1)S(1)}, u32[]{:S(2)}, u32[]{:S(2)}) collective-permute-start(bf16[1,2,1024]{2,1,0:T(2,128)(2,1)S(1)} %get-tuple-element.23), channel_id=1, source_target_pairs={{0,8},{1,9},{2,10},{3,11},{4,12},{5,13},{6,14},{7,15},{8,0},{9,1},... | collective-permute-start | bytes 12296 | tf_op jit(solution)/shard_map/ppermute | solution.py:31
  163.6 9.9 %collective-permute-start.23 = (bf16[1,2,1024]{2,1,0:T(2,128)(2,1)S(1)}, bf16[1,2,1024]{2,1,0:T(2,128)(2,1)S(1)}, u32[]{:S(2)}, u32[]{:S(2)}) collective-permute-start(bf16[1,2,1024]{2,1,0:T(2,128)(2,1)S(1)} %get-tuple-element.22), channel_id=1, source_target_pairs={{0,9},{1,8},{2,11},{3,10},{4,13},{5,12},{6,15},{7,14},{8,1},{9,0},... | collective-permute-start | bytes 12296 | tf_op jit(solution)/shard_map/ppermute | solution.py:31
  166.0 8.2 %collective-permute-start.24 = (bf16[1,2,1024]{2,1,0:T(2,128)(2,1)S(1)}, bf16[1,2,1024]{2,1,0:T(2,128)(2,1)S(1)}, u32[]{:S(2)}, u32[]{:S(2)}) collective-permute-start(bf16[1,2,1024]{2,1,0:T(2,128)(2,1)S(1)} %get-tuple-element.21), channel_id=1, source_target_pairs={{0,10},{1,11},{2,8},{3,9},{4,14},{5,15},{6,12},{7,13},{8,2},{9,3},... | collective-permute-start | bytes 12296 | tf_op jit(solution)/shard_map/ppermute | solution.py:31
  166.5 11.7 %collective-permute-start.25 = (bf16[1,2,1024]{2,1,0:T(2,128)(2,1)S(1)}, bf16[1,2,1024]{2,1,0:T(2,128)(2,1)S(1)}, u32[]{:S(2)}, u32[]{:S(2)}) collective-permute-start(bf16[1,2,1024]{2,1,0:T(2,128)(2,1)S(1)} %get-tuple-element.20), channel_id=1, source_target_pairs={{0,11},{1,10},{2,9},{3,8},{4,15},{5,14},{6,13},{7,12},{8,3},{9,2},... | collective-permute-start | bytes 12296 | tf_op jit(solution)/shard_map/ppermute | solution.py:31
  169.8 8.4 %collective-permute-start.26 = (bf16[1,2,1024]{2,1,0:T(2,128)(2,1)S(1)}, bf16[1,2,1024]{2,1,0:T(2,128)(2,1)S(1)}, u32[]{:S(2)}, u32[]{:S(2)}) collective-permute-start(bf16[1,2,1024]{2,1,0:T(2,128)(2,1)S(1)} %get-tuple-element.19), channel_id=1, source_target_pairs={{0,12},{1,13},{2,14},{3,15},{4,8},{5,9},{6,10},{7,11},{8,4},{9,5},... | collective-permute-start | bytes 12296 | tf_op jit(solution)/shard_map/ppermute | solution.py:31
  170.4 7.8 %collective-permute-start.27 = (bf16[1,2,1024]{2,1,0:T(2,128)(2,1)S(1)}, bf16[1,2,1024]{2,1,0:T(2,128)(2,1)S(1)}, u32[]{:S(2)}, u32[]{:S(2)}) collective-permute-start(bf16[1,2,1024]{2,1,0:T(2,128)(2,1)S(1)} %get-tuple-element.18), channel_id=1, source_target_pairs={{0,13},{1,12},{2,15},{3,14},{4,9},{5,8},{6,11},{7,10},{8,5},{9,4},... | collective-permute-start | bytes 12296 | tf_op jit(solution)/shard_map/ppermute | solution.py:31
  173.5 6.4 %collective-permute-start.28 = (bf16[1,2,1024]{2,1,0:T(2,128)(2,1)S(1)}, bf16[1,2,1024]{2,1,0:T(2,128)(2,1)S(1)}, u32[]{:S(2)}, u32[]{:S(2)}) collective-permute-start(bf16[1,2,1024]{2,1,0:T(2,128)(2,1)S(1)} %get-tuple-element.17), channel_id=1, source_target_pairs={{0,14},{1,15},{2,12},{3,13},{4,10},{5,11},{6,8},{7,9},{8,6},{9,7},... | collective-permute-start | bytes 12296 | tf_op jit(solution)/shard_map/ppermute | solution.py:31
  174.3 5.8 %collective-permute-start.29 = (bf16[1,2,1024]{2,1,0:T(2,128)(2,1)S(1)}, bf16[1,2,1024]{2,1,0:T(2,128)(2,1)S(1)}, u32[]{:S(2)}, u32[]{:S(2)}) collective-permute-start(bf16[1,2,1024]{2,1,0:T(2,128)(2,1)S(1)} %get-tuple-element.16), channel_id=1, source_target_pairs={{0,15},{1,14},{2,13},{3,12},{4,11},{5,10},{6,9},{7,8},{8,7},{9,6},... | collective-permute-start | bytes 12296 | tf_op jit(solution)/shard_map/ppermute | solution.py:31
  180.4 3.3 %copy-start.9 = (bf16[1,32,1500]{2,1,0:T(8,128)(2,1)S(1)}, bf16[1,32,1500]{2,1,0:T(8,128)(2,1)}, u32[]{:S(2)}) copy-start(bf16[1,32,1500]{2,1,0:T(8,128)(2,1)} %copy-done.8) | copy-start | bytes 288004
